TPU v7x, 32 devices: a whole 2x2x4 slice. The times are simulated.
32 devices in a mesh: space: 8 (over y, x, core), tm: 4 (over z).
Axes of the slice: x: 2, y: 2, z: 4, core: 2. Of those that a mesh axis runs over, the one named last changes fastest.
Arguments:
- residual_in: float32 [32768, 2048], P('space', 'tm'), may hold values from -6 to 6
- factor_panel: float32 [32768, 1024], P('space'), may hold values from -0.1875 to 0.1875
- diag_inverse: float32 [4, 256, 256], replicated, may hold values from -2 to 2, as said below
- time_inverse: float32 [2048, 2048], P('space'), may hold values from -2 to 2, as said below
Outputs:
- whitened: float32 [32768, 2048], P(('space', 'tm'))
Inputs may be any that keep to these rules, and one draw needn't show every extreme that they name: `diag_inverse`: lower triangular, with diagonal entries between 0.5 and 2. `time_inverse`: lower triangular, with diagonal entries between 0.5 and 2.
All inputs are finite; a program needn't handle non-finite values.
Results may differ from a plain program's by a relative error of at most 0.0001.
Values sent between devices are 32-bit elements; how exact they have to be, the bound alone decides.
No kernel may reach another device: no remote copies, remote signals or barrier semaphores. Data moves between devices by JAX's collectives and lax.ppermute only.
A program may use at most 128 MiB of HBM per device.

v0:
```python
import jax
import jax.numpy as jnp
from jax import lax
from jax.sharding import PartitionSpec as P


def broadcast(block, axis, owner):
    block = jnp.where(lax.axis_index(axis) == owner, block, jnp.zeros_like(block))
    return lax.psum(block, axis)


def product(left, right):
    return jnp.dot(left, right, precision=lax.Precision.HIGHEST, preferred_element_type=jnp.float32)


def product_by_rows(left, right):
    return lax.dot_general(
        left,
        right,
        (((1,), (1,)), ((), ())),
        precision=lax.Precision.HIGHEST,
        preferred_element_type=jnp.float32,
    )


def share(candidate, current):
    return broadcast(candidate, "space", current)


def shards(residual_in, factor_panel, diag_inverse, time_inverse):
    width = diag_inverse.shape[1]
    steps_total = diag_inverse.shape[0]
    position = lax.axis_index("space")
    head_rows = residual_in[:width]
    tail_rows = residual_in[width:]
    candidate = product(diag_inverse[0], head_rows)
    for current in range(steps_total):
        solved = share(candidate, current)
        columns = factor_panel[:, current * width : (current + 1) * width]
        head_rows = jnp.where(
            position > current,
            head_rows - product(columns[:width], solved),
            jnp.where(position == current, solved, head_rows),
        )
        if current + 1 < steps_total:
            candidate = product(diag_inverse[current + 1], head_rows)
        tail_rows = tail_rows - product(columns[width:], solved)
    values = jnp.concatenate([head_rows, tail_rows], 0)
    turned = lax.all_to_all(values, "tm", split_axis=0, concat_axis=1, tiled=True)
    return product_by_rows(turned, lax.all_gather(time_inverse, "space", axis=0, tiled=True))


def solution(mesh):
    in_specs = (P("space", "tm"), P("space", None), P(), P("space", None))
    out_specs = P(("space", "tm"), None)
    return jax.shard_map(shards, mesh=mesh, in_specs=in_specs, out_specs=out_specs, check_vma=False)
```

profile of v0, /device:TPU:0, one launch (start us, length us, event | category | flops | bytes accessed | tf_op | source)
XLA Modules:
  0.0 592.7 jit_solution(16608482617738462351)
XLA Ops:
  6.5 0.0 all-reduce.5.cloned.1.call-start
  6.5 2.5 convolution_select_fusion.3
  9.1 0.0 all-reduce.5.cloned.1.call-update
  9.1 0.0 all-reduce.7.cloned.1.call-start
  9.1 58.8 %all-reduce.5.cloned.1.call-done = f32[256,512]{1,0:T(8,128)} async-done(((f32[256,512]{1,0:T(8,128)}), f32[256,512]{1,0:T(8,128)}) %all-reduce.5.cloned.1.call-update) | async-done | bytes 524304 | tf_op jit(solution)/shard_map/psum | solution.py:9
  68.0 2.1 fusion.11
  70.1 2.4 fusion.9
  72.5 0.0 all-reduce.7.cloned.1.call-update
  72.5 0.0 all-reduce.9.cloned.1.call-start
  72.6 54.2 %all-reduce.7.cloned.1.call-done = f32[256,512]{1,0:T(8,128)} async-done(((f32[256,512]{1,0:T(8,128)}), f32[256,512]{1,0:T(8,128)}) %all-reduce.7.cloned.1.call-update) | async-done | bytes 524304 | tf_op jit(solution)/shard_map/psum | solution.py:9
  126.8 2.0 fusion.13
  128.7 2.4 fusion.8
  131.1 0.0 all-reduce.9.cloned.1.call-update
  131.2 0.0 all-reduce.11.cloned.1.call-start
  131.2 54.2 %all-reduce.9.cloned.1.call-done = f32[256,512]{1,0:T(8,128)} async-done(((f32[256,512]{1,0:T(8,128)}), f32[256,512]{1,0:T(8,128)}) %all-reduce.9.cloned.1.call-update) | async-done | bytes 524304 | tf_op jit(solution)/shard_map/psum | solution.py:9
  185.4 2.0 fusion.15
  187.4 2.4 fusion.7
  189.8 0.0 all-reduce.11.cloned.1.call-update
  189.8 0.3 all-gather.2.cloned.1.call-start
  190.2 0.2 all-gather.2.cloned.1.call-update
  190.4 7.4 %slice.63 = f32[3840,512]{1,0:T(8,128)} slice(f32[4096,512]{1,0:T(8,128)} %param.4), slice={[256:4096], [0:512]} | slice | bytes 15728640 | tf_op jit(solution)/shard_map/slice | solution.py:35
  197.8 9.2 %copy.19 = f32[3840,512]{0,1:T(8,128)} copy(f32[3840,512]{1,0:T(8,128)} %slice.63) | data formatting | bytes 15728640
  207.0 17.2 %fusion.5 = f32[512,3840]{1,0:T(8,128)} fusion(f32[256,512]{1,0:T(8,128)S(1)} %copy-done, f32[4096,1024]{1,0:T(8,128)} %param.5), kind=kOutput, calls=%fused_computation.11 | convolution fusion | flops 6039797760 | bytes 12320768 | tf_op jit(solution)/shard_map/dot_general | solution.py:13
  224.1 17.5 %fusion.3 = f32[512,3840]{1,0:T(8,128)} fusion(f32[256,512]{1,0:T(8,128)S(1)} %copy-done.1, f32[4096,1024]{1,0:T(8,128)} %param.5), kind=kOutput, calls=%fused_computation.9 | convolution fusion | flops 6039797760 | bytes 12320768 | tf_op jit(solution)/shard_map/dot_general | solution.py:13
  241.7 17.2 %fusion.1 = f32[512,3840]{1,0:T(8,128)} fusion(f32[256,512]{1,0:T(8,128)S(1)} %copy-done.2, f32[4096,1024]{1,0:T(8,128)} %param.5), kind=kOutput, calls=%fused_computation.7 | convolution fusion | flops 6039797760 | bytes 12320768 | tf_op jit(solution)/shard_map/dot_general | solution.py:13
  258.9 2.0 fusion.17
  260.9 1.0 copy.14
  261.9 23.3 %bitcast_subtract_fusion = f32[3840,512]{0,1:T(8,128)S(1)} fusion(f32[512,3840]{1,0:T(8,128)} %fusion.1, f32[512,3840]{1,0:T(8,128)} %fusion.3, f32[3840,512]{0,1:T(8,128)} %copy.19, f32[512,3840]{1,0:T(8,128)} %fusion.5, f32[256,512]{1,0:T(8,128)} %all-reduce.11.cloned.1.call-done, f32[4096,1024]{1,0:T(8,128)} %param.5), kind=kOutput, calls=%fused_computation.2 | convolution fusion | flops 6047662080 | bytes 43778048 | tf_op jit(solution)/shard_map/dot_general | solution.py:13
  285.2 2.2 pad_maximum_fusion
  287.4 1.7 copy.22
  289.1 186.6 %all_to_all.19 = f32[4,1024,512]{1,2,0:T(8,128)} all-to-all(f32[4,1024,512]{1,2,0:T(8,128)S(1)} %bitcast.77), channel_id=1, replica_groups=mesh['space'=8,'tm'=4] {'tm'}, dimensions={0} | all-to-all | bytes 16777216 | tf_op jit(solution)/shard_map/all_to_all | solution.py:49
  475.7 110.2 %fusion.31 = f32[1024,2048]{1,0:T(8,128)} fusion(f32[1024,2048]{0,1:T(8,128)} %bitcast.78, f32[2048,2048]{1,0:T(8,128)} %all-gather.2.cloned.1.call-done), kind=kOutput, calls=%fused_computation.45 | convolution fusion | flops 51539607552 | bytes 33554432 | tf_op jit(solution)/shard_map/dot_general | solution.py:17
  (8 shorter events, 0.0 us)
Async XLA Ops:
  6.5 61.4 %all-reduce.5.cloned.1.call-start = ((), (), s32[]{:S(2)}) async-start(), calls=%async_computation.1 | async-start | bytes 1048576 | tf_op jit(solution)/shard_map/psum | solution.py:9
  9.1 117.7 %all-reduce.7.cloned.1.call-start = ((), (), s32[]{:S(2)}) async-start(), calls=%async_computation.2 | async-start | bytes 1048576 | tf_op jit(solution)/shard_map/psum | solution.py:9
  72.5 112.9 %all-reduce.9.cloned.1.call-start = ((), (), s32[]{:S(2)}) async-start(), calls=%async_computation.3 | async-start | bytes 1048576 | tf_op jit(solution)/shard_map/psum | solution.py:9
  131.2 127.8 %all-reduce.11.cloned.1.call-start = ((), (), s32[]{:S(2)}) async-start(), calls=%async_computation.4 | async-start | bytes 1048576 | tf_op jit(solution)/shard_map/psum | solution.py:9
  189.8 285.9 %all-gather.2.cloned.1.call-start = ((), (), s32[]{:S(2)}) async-start(), calls=%async_computation.5 | async-start | bytes 18874368 | tf_op jit(solution)/shard_map/all_gather | solution.py:50
  197.8 9.2 %copy-start = (f32[256,512]{1,0:T(8,128)S(1)}, f32[256,512]{1,0:T(8,128)}, u32[]{:S(2)}) copy-start(f32[256,512]{1,0:T(8,128)} %all-reduce.5.cloned.1.call-done) | copy-start | bytes 1572868
  207.0 17.2 %copy-start.1 = (f32[256,512]{1,0:T(8,128)S(1)}, f32[256,512]{1,0:T(8,128)}, u32[]{:S(2)}) copy-start(f32[256,512]{1,0:T(8,128)} %all-reduce.7.cloned.1.call-done) | copy-start | bytes 1572868
  224.1 17.6 %copy-start.2 = (f32[256,512]{1,0:T(8,128)S(1)}, f32[256,512]{1,0:T(8,128)}, u32[]{:S(2)}) copy-start(f32[256,512]{1,0:T(8,128)} %all-reduce.9.cloned.1.call-done) | copy-start | bytes 1572868
Sparse Core Ops, SparseCore 0:
  10.4 57.4 all-reduce.4
  72.6 54.1 all-reduce.6
  131.3 54.0 all-reduce.8
  189.9 54.0 all-reduce.10
  245.8 89.0 all-gather.1
where the time goes:
time: 597 us; the launch traced here: 593 us
  matrix products  203 us (34%)
  blocking collectives  187 us (31%)
  waiting for transfers between devices  168 us (28%)
  local copies, waits for them, and re-layouts  19.2 us (3%)
  between operations  13.5 us (2%)
    all_to_all x1, blocking collectives, shards(): lax.all_to_all(values, 'tm', split_axis=0, concat_axis=1, tiled=True)  187 us
    psum x4, waiting for transfers between devices, broadcast(): return lax.psum(block, axis)  167 us
    dot_general x1, matrix products, product_by_rows(): lax.dot_general(left, right, (((1,), (1,)), ((), ())), precision=lax.Prec...  110 us
    dot_general x12, matrix products, product(): jnp.dot(left, right, precision=lax.Precision.HIGHEST, preferred_element_t...  93 us
  transfers between devices with their start and end apart: 5, of which 3 were waited for; matrix products, arithmetic and copies ran while one was open for 17% of the time, Pallas kernels for 0%

commit v1 on v0

--- a/solution.py
+++ b/solution.py
@@ -6,7 +6,7 @@
 
 def broadcast(block, axis, owner):
     block = jnp.where(lax.axis_index(axis) == owner, block, jnp.zeros_like(block))
-    return lax.psum(block, axis)
+    return jnp.sum(lax.all_gather(block, axis), axis=0)
 
 
 def product(left, right):

time: 597 us -> 555 us (0.930)
  blocking collectives: 187 us -> 0 us
  waiting for transfers between devices: 168 us -> 299 us
  matrix products: 203 us -> 186 us
  local copies, waits for them, and re-layouts: 19.2 us -> 34.9 us
  other arithmetic: 2.21 us -> 8.55 us
    all_to_all x1 -> x0, blocking collectives: 187 us -> none  [shards(): lax.all_to_all(values, 'tm', split_axis=0, concat_axis=1, tiled=True)]
    psum x4 -> x0, waiting for transfers between devices: 167 us -> none  [broadcast(): return lax.psum(block, axis)]
    all_to_all x0 -> x1, waiting for transfers between devices: none -> 151 us  [shards(): lax.all_to_all(values, 'tm', split_axis=0, concat_axis=1, tiled=True)]
    all_gather x0 -> x4, waiting for transfers between devices: none -> 114 us  [broadcast(): return jnp.sum(lax.all_gather(block, axis), axis=0)]
    all_gather x1, waiting for transfers between devices: 0.01 us -> 32.9 us  [shards(): lax.all_gather(time_inverse, 'space', axis=0, tiled=True)]
    dot_general x12, matrix products: 93 us -> 76.1 us  [product(): jnp.dot(left, right, precision=lax.Precision.HIGHEST, preferred_element_t...]
    unnamed x7 -> x6, local copies, waits for them, and re-layouts: 9.22 us -> 21.7 us
    reduce_sum x0 -> x4, other arithmetic: none -> 6.5 us  [broadcast(): return jnp.sum(lax.all_gather(block, axis), axis=0)]
  transfers between devices with their start and end apart: 5 -> 6, of which waited for: 3 -> 5; matrix products, arithmetic and copies ran while one was open for 17% -> 16% of each run, Pallas kernels for 0% -> 0%
where the time goes in v1:
time: 555 us; the launch traced here: 548 us
  waiting for transfers between devices  299 us (54%)
  matrix products  186 us (34%)
  local copies, waits for them, and re-layouts  34.9 us (6%)
  between operations  13.5 us (2%)
  other arithmetic  8.55 us (2%)
  starting transfers between devices  6 us (1%)
    all_to_all x1, waiting for transfers between devices, shards(): lax.all_to_all(values, 'tm', split_axis=0, concat_axis=1, tiled=True)  151 us
    all_gather x4, waiting for transfers between devices, broadcast(): return jnp.sum(lax.all_gather(block, axis), axis=0)  114 us
    dot_general x1, matrix products, product_by_rows(): lax.dot_general(left, right, (((1,), (1,)), ((), ())), precision=lax.Prec...  110 us
    dot_general x12, matrix products, product(): jnp.dot(left, right, precision=lax.Precision.HIGHEST, preferred_element_t...  76.1 us
    all_gather x1, waiting for transfers between devices, shards(): lax.all_gather(time_inverse, 'space', axis=0, tiled=True)  32.9 us
    unnamed x6, local copies, waits for them, and re-layouts  21.7 us
  transfers between devices with their start and end apart: 6, of which 5 were waited for; matrix products, arithmetic and copies ran while one was open for 16% of the time, Pallas kernels for 0%

profile of v1, /device:TPU:0, one launch (start us, length us, event | category | flops | bytes accessed | tf_op | source)
XLA Modules:
  0.0 548.1 jit_solution(1220955469861362677)
XLA Ops:
  6.5 2.5 convolution_select_fusion.3
  9.1 39.4 %all-gather.12.cloned.1.call-done = f32[2048,512]{1,0:T(8,128)} async-done(((f32[256,512]{1,0:T(8,128)}), f32[2048,512]{1,0:T(8,128)}) %all-gather.12.cloned.1.call-update) | async-done | bytes 4194320 | tf_op jit(solution)/shard_map/all_gather | solution.py:9
  48.6 2.7 reduce_sum.36
  51.3 1.8 fusion.11
  53.1 2.7 fusion.9
  55.9 37.4 %all-gather.14.cloned.1.call-done = f32[2048,512]{0,1:T(8,128)} async-done(((f32[256,512]{0,1:T(8,128)}), f32[2048,512]{0,1:T(8,128)}) %all-gather.14.cloned.1.call-update) | async-done | bytes 4194320 | tf_op jit(solution)/shard_map/all_gather | solution.py:9
  93.3 4.1 copy.18
  97.5 1.3 bitcast_reduce_fusion.2
  99.0 1.6 fusion.13
  100.6 2.7 fusion.8
  103.6 37.3 %all-gather.16.cloned.1.call-done = f32[2048,512]{0,1:T(8,128)} async-done(((f32[256,512]{0,1:T(8,128)}), f32[2048,512]{0,1:T(8,128)}) %all-gather.16.cloned.1.call-update) | async-done | bytes 4194320 | tf_op jit(solution)/shard_map/all_gather | solution.py:9
  140.9 4.1 copy.19
  145.0 1.3 bitcast_reduce_fusion.1
  146.5 1.6 fusion.15
  148.1 2.7 fusion.7
  151.0 0.5 all-gather.10.cloned.1.call-update
  151.5 7.4 %slice.63 = f32[3840,512]{1,0:T(8,128)} slice(f32[4096,512]{1,0:T(8,128)} %param.4), slice={[256:4096], [0:512]} | slice | bytes 15728640 | tf_op jit(solution)/shard_map/slice | solution.py:35
  158.9 9.3 %copy.16 = f32[3840,512]{0,1:T(8,128)} copy(f32[3840,512]{1,0:T(8,128)} %slice.63) | data formatting | bytes 15728640
  168.1 17.0 %fusion.5 = f32[512,3840]{1,0:T(8,128)} fusion(f32[256,512]{1,0:T(8,128)S(1)} %reduce_sum.36, f32[4096,1024]{1,0:T(8,128)} %param.5), kind=kOutput, calls=%fused_computation.14 | convolution fusion | flops 6039797760 | bytes 12320768 | tf_op jit(solution)/shard_map/dot_general | solution.py:13
  185.2 11.0 %fusion.3 = f32[512,3840]{1,0:T(8,128)} fusion(f32[256,512]{0,1:T(8,128)S(1)} %bitcast_reduce_fusion.2, f32[4096,1024]{1,0:T(8,128)} %param.5), kind=kOutput, calls=%fused_computation.12 | convolution fusion | flops 6039797760 | bytes 12320768 | tf_op jit(solution)/shard_map/dot_general | solution.py:13
  196.2 12.1 %fusion.1 = f32[512,3840]{1,0:T(8,128)} fusion(f32[256,512]{0,1:T(8,128)S(1)} %bitcast_reduce_fusion.1, f32[4096,1024]{1,0:T(8,128)} %param.5), kind=kOutput, calls=%fused_computation.10 | convolution fusion | flops 6039797760 | bytes 12320768 | tf_op jit(solution)/shard_map/dot_general | solution.py:13
  208.3 4.1 copy.20
  212.4 1.3 bitcast_reduce_fusion
  213.9 1.6 fusion.17
  215.6 1.0 copy.14
  216.6 18.5 %bitcast_subtract_fusion = f32[3840,512]{0,1:T(8,128)S(1)} fusion(f32[512,3840]{1,0:T(8,128)} %fusion.1, f32[512,3840]{1,0:T(8,128)} %fusion.3, f32[3840,512]{0,1:T(8,128)} %copy.16, f32[512,3840]{1,0:T(8,128)} %fusion.5, f32[256,512]{0,1:T(8,128)} %copy-done, f32[4096,1024]{1,0:T(8,128)} %param.5), kind=kOutput, calls=%fused_computation.2 | convolution fusion | flops 6047662080 | bytes 43778048 | tf_op jit(solution)/shard_map/dot_general | solution.py:13
  235.0 2.0 pad_maximum_fusion
  237.1 4.2 copy.22
  241.3 5.7 %all-to-all-start = ((f32[4,1024,512]{1,2,0:T(8,128)}), f32[4,1024,512]{1,2,0:T(8,128)}, u32[]{:S(2)}, u32[]{:S(2)}) async-start(f32[4,1024,512]{1,2,0:T(8,128)} %bitcast.92), calls=%async_computation | async-start | bytes 16777216 | tf_op jit(solution)/shard_map/all_to_all | solution.py:49
  247.0 32.9 %all-gather.10.cloned.1.call-done = f32[2048,2048]{1,0:T(8,128)} async-done(((f32[256,2048]{1,0:T(8,128)}), f32[2048,2048]{1,0:T(8,128)}) %all-gather.10.cloned.1.call-update) | async-done | bytes 16777232 | tf_op jit(solution)/shard_map/all_gather | solution.py:50
  279.9 151.3 %all-to-all-done = f32[4,1024,512]{1,2,0:T(8,128)} async-done(((f32[4,1024,512]{1,2,0:T(8,128)}), f32[4,1024,512]{1,2,0:T(8,128)}, u32[]{:S(2)}, u32[]{:S(2)}) %all-to-all-start) | async-done | bytes 8388640 | tf_op jit(solution)/shard_map/all_to_all | solution.py:49
  431.2 110.1 %fusion.31 = f32[1024,2048]{1,0:T(8,128)} fusion(f32[1024,2048]{0,1:T(8,128)} %bitcast.17, f32[2048,2048]{1,0:T(8,128)} %all-gather.10.cloned.1.call-done), kind=kOutput, calls=%fused_computation.48 | convolution fusion | flops 51539607552 | bytes 33554432 | tf_op jit(solution)/shard_map/dot_general | solution.py:17
  (15 shorter events, 1.0 us)
Async XLA Ops:
  6.5 42.0 %all-gather.12.cloned.1.call-start = ((), (), s32[]{:S(2)}) async-start(), calls=%async_computation.2 | async-start | bytes 4718592 | tf_op jit(solution)/shard_map/all_gather | solution.py:9
  9.1 84.2 %all-gather.14.cloned.1.call-start = ((), (), s32[]{:S(2)}) async-start(), calls=%async_computation.3 | async-start | bytes 4718592 | tf_op jit(solution)/shard_map/all_gather | solution.py:9
  55.8 85.0 %all-gather.16.cloned.1.call-start = ((), (), s32[]{:S(2)}) async-start(), calls=%async_computation.4 | async-start | bytes 4718592 | tf_op jit(solution)/shard_map/all_gather | solution.py:9
  103.4 104.9 %all-gather.18.cloned.1.call-start = ((), (), s32[]{:S(2)}) async-start(), calls=%async_computation.5 | async-start | bytes 4718592 | tf_op jit(solution)/shard_map/all_gather | solution.py:9
  150.9 129.0 %all-gather.10.cloned.1.call-start = ((), (), s32[]{:S(2)}) async-start(), calls=%async_computation.1 | async-start | bytes 18874368 | tf_op jit(solution)/shard_map/all_gather | solution.py:50
  213.7 1.9 copy-start
  241.3 189.9 %all-to-all-start = ((f32[4,1024,512]{1,2,0:T(8,128)}), f32[4,1024,512]{1,2,0:T(8,128)}, u32[]{:S(2)}, u32[]{:S(2)}) async-start(f32[4,1024,512]{1,2,0:T(8,128)} %bitcast.92), calls=%async_computation | async-start | bytes 16777216 | tf_op jit(solution)/shard_map/all_to_all | solution.py:49
Sparse Core Ops, SparseCore 0:
  9.2 39.2 all-gather.11
  56.0 37.3 all-gather.13
  103.5 37.3 all-gather.15
  151.0 37.3 all-gather.17
  190.1 89.7 all-gather.9
